TPU v7x, 256 devices: a whole 4x4x8 slice. The times are simulated.
256 devices in a mesh: scen: 16 (over z_lo, y, core), tm: 16 (over z_hi, x).
Axes of the slice: x: 4, y: 4, z: 8 (z_hi: 4, z_lo: 2; z = z_hi * 2 + z_lo), core: 2. Of those that a mesh axis runs over, the one named last changes fastest.
Arguments:
- cotangent: float32 [64, 336, 2048], P('scen', 'tm'), may hold values from -6 to 6
- blocks: bfloat16 [16, 6, 128, 128], P('tm'), may hold values from -0.21875 to 0.21875
- zone_links: int32 [16, 6], replicated, may hold values from 0 to 15, as said below
- step_size: float32 [2048], replicated, may hold values from 0.3 to 1
- coupling: bfloat16 [16, 336, 336], P('tm'), may hold values from -0.3125 to 0.3125
- ramp_band: int32 [16], P('tm'), may hold values from 42 to 336, as said below
- candidates: int32 [2048], P('scen'), may hold values from 0 to 2047, as said below
Outputs:
- initial_adjoint: float32 [64, 336, 2048], P('scen', 'tm')
- siting_gradient: float32 [336, 2048], P('tm', 'scen')
Inputs may be any that keep to these rules, and one draw needn't show every extreme that they name: zone_links[z, 0] = z, and the 6 entries of a row are distinct zones. `ramp_band`: at least one zone has reach 336. `candidates`: the entries of block m of 128 consecutive entries are distinct buses in m * (128) to (m + 1) * 128 - 1.
All inputs are finite; a program needn't handle non-finite values.
Results may differ from a plain program's by a relative error of at most 0.0029.
Values may be sent and summed in bfloat16 or wider, within the bound.
No kernel may reach another device: no remote copies, remote signals or barrier semaphores. Data moves between devices by JAX's collectives and lax.ppermute only.
A program may use at most 64 MiB of HBM per device.

v0:
```python
import jax
import jax.numpy as jnp
from jax import lax
from jax.sharding import PartitionSpec as P

SWEEPS = 2


def network_term(scaled, link_blocks, zone_links):
    scen_count, hour_count, buses = scaled.shape
    link_count, zone_count, bus_width = (
        link_blocks.shape[0],
        link_blocks.shape[1],
        link_blocks.shape[3],
    )
    zone_major = jnp.transpose(
        scaled.reshape(scen_count * hour_count, zone_count, bus_width), (1, 0, 2)
    )
    total = jnp.zeros((zone_count, scen_count * hour_count, bus_width), jnp.float32)
    for link in range(link_count):
        picked = jnp.take(zone_major, zone_links[:, link], axis=0)
        total = total + lax.dot_general(
            picked,
            link_blocks[link],
            (((2,), (1,)), ((0,), (0,))),
            preferred_element_type=jnp.float32,
        )
    return jnp.transpose(total, (1, 0, 2)).reshape(scen_count, hour_count, buses)


def temporal_term(moved, masked_turned):
    scen_count, hour_count, owned = moved.shape
    zone_count = masked_turned.shape[0]
    bus_width = owned // zone_count
    rows = []
    for scen in range(scen_count):
        column = moved[scen, :, 0:bus_width]
        pieces = jnp.dot(masked_turned[0], column, preferred_element_type=jnp.float32)
        rows.append(pieces)
    return jnp.stack(rows, axis=0).astype(jnp.bfloat16)


def per_device(cotangent, blocks, zone_links, step_size, coupling, ramp_band, candidates):
    all_blocks = lax.all_gather(blocks, "tm", axis=0, tiled=True)
    link_blocks = jnp.transpose(all_blocks, (1, 0, 2, 3))
    hour_count = coupling.shape[1]
    hour_ids = jnp.arange(hour_count, dtype=jnp.int32)
    spread = jnp.abs(hour_ids[:, None] - hour_ids[None, :])
    masked = jnp.where(
        spread[None, :, :] <= ramp_band[:, None, None], coupling, jnp.zeros_like(coupling)
    )
    masked_turned = jnp.transpose(masked, (0, 2, 1))
    scen_total = cotangent.shape[0] * lax.axis_size("scen")
    adjoint = cotangent
    grad_local = jnp.zeros((cotangent.shape[1], cotangent.shape[2]), jnp.float32)
    for sweep in range(SWEEPS):
        weighted = adjoint * step_size[None, None, :]
        sweep_grad = jnp.sum(weighted, axis=0) * (1.0 / scen_total)
        grad_local = grad_local + sweep_grad
        scaled = weighted.astype(jnp.bfloat16)
        moved = lax.all_to_all(scaled, "tm", split_axis=2, concat_axis=1, tiled=True)
        temporal = lax.all_to_all(
            temporal_term(moved, masked_turned), "tm", split_axis=1, concat_axis=2, tiled=True
        )
        network = network_term(scaled, link_blocks, zone_links)
        adjoint = adjoint - network - temporal.astype(jnp.float32)
    reduced = lax.psum_scatter(grad_local, "scen", scatter_dimension=1, tiled=True)
    width = reduced.shape[1]
    local_cols = candidates - lax.axis_index("scen") * width
    siting_gradient = jnp.take(reduced, local_cols, axis=1)
    return (adjoint, siting_gradient)


def solution(mesh):
    placed = (
        P("scen", "tm", None),
        P("tm", None, None, None),
        P(),
        P(),
        P("tm", None, None),
        P("tm"),
        P("scen"),
    )
    return jax.shard_map(
        per_device,
        mesh=mesh,
        in_specs=placed,
        out_specs=(P("scen", "tm", None), P("tm", "scen")),
        check_vma=False,
    )
```

profile of v0, /device:TPU:24, one launch (start us, length us, event | category | flops | bytes accessed | tf_op | source)
XLA Modules:
  0.0 205.9 jit_solution(9475349268298341223)
XLA Ops:
  10.9 4.2 %reshape.228 = bf16[16,2,5376]{2,1,0:T(2,128)(2,1)} reshape(bf16[2048,4,21]{2,1,0:T(4,128)(2,1)S(1)} %bitcast.148) | data formatting | bytes 688128
  15.0 11.0 %all-to-all-start = ((bf16[16,2,5376]{2,1,0:T(2,128)(2,1)}), bf16[16,2,5376]{2,1,0:T(2,128)(2,1)S(1)}, u32[]{:S(2)}, u32[]{:S(2)}) async-start(bf16[16,2,5376]{2,1,0:T(2,128)(2,1)} %reshape.228), calls=%async_computation | async-start | bytes 688128 | tf_op jit(solution)/shard_map/all_to_all | solution.py:61
  27.2 14.7 %all-to-all-done = bf16[16,2,5376]{2,1,0:T(2,128)(2,1)S(1)} async-done(((bf16[16,2,5376]{2,1,0:T(2,128)(2,1)}), bf16[16,2,5376]{2,1,0:T(2,128)(2,1)S(1)}, u32[]{:S(2)}, u32[]{:S(2)}) %all-to-all-start) | async-done | bytes 344096 | tf_op jit(solution)/shard_map/all_to_all | solution.py:61
  41.9 5.1 %reshape.229 = bf16[2048,4,21]{2,1,0:T(4,128)(2,1)S(1)} reshape(bf16[16,2,5376]{2,1,0:T(2,128)(2,1)S(1)} %all-to-all-done) | data formatting | bytes 688128
  50.9 6.2 %all-to-all-start.1 = ((bf16[4,336,128]{2,0,1:T(4,128)(2,1)}), bf16[4,336,128]{2,0,1:T(4,128)(2,1)S(1)}, u32[]{:S(2)}, u32[]{:S(2)}) async-start(bf16[4,336,128]{2,0,1:T(4,128)(2,1)} %copy.93), calls=%async_computation.1 | async-start | bytes 688128 | tf_op jit(solution)/shard_map/all_to_all | solution.py:62
  65.9 6.9 %all-to-all-done.1 = bf16[4,336,128]{2,0,1:T(4,128)(2,1)S(1)} async-done(((bf16[4,336,128]{2,0,1:T(4,128)(2,1)}), bf16[4,336,128]{2,0,1:T(4,128)(2,1)S(1)}, u32[]{:S(2)}, u32[]{:S(2)}) %all-to-all-start.1) | async-done | bytes 344096 | tf_op jit(solution)/shard_map/all_to_all | solution.py:62
  73.9 13.9 %all-gather.2.cloned.1.call-done = bf16[16,6,128,128]{3,2,0,1:T(8,128)(2,1)} async-done(((bf16[1,6,128,128]{3,2,0,1:T(8,128)(2,1)}), bf16[16,6,128,128]{3,2,0,1:T(8,128)(2,1)}) %all-gather.2.cloned.1.call-update) | async-done | bytes 3145744 | tf_op jit(solution)/shard_map/all_gather | solution.py:44
  87.8 1.7 fusion.15
  94.8 2.1 %reshape.78 = f32[4,21,2048]{2,1,0:T(8,128)} reshape(f32[84,16,128]{2,1,0:T(8,128)} %copy.85) | data formatting | bytes 1376256 | tf_op jit(solution)/shard_map/reshape | solution.py:28
  96.9 2.9 %multiply_reduce_fusion = (f32[21,2048]{1,0:T(8,128)}, f32[21,2048]{1,0:T(8,128)}, f32[4,21,2048]{2,1,0:T(8,128)S(1)}) fusion(f32[2048]{0:T(1024)S(1)} %copy-done.7, f32[4,21,2048]{2,0,1:T(4,128)} %param.9, f32[4,21,2048]{2,1,0:T(8,128)} %reshape.226, f32[4,21,2048]{2,1,0:T(8,128)} %reshape.78), kind=kLoop, calls=%fused_computation.47 | loop fusion | flops 946176 | bytes 3104768 | tf_op jit(solution)/shard_map/reduce_sum | solution.py:58
  109.3 4.0 %copy.98 = bf16[4,21,2048]{1,0,2:T(4,128)(2,1)} copy(bf16[4,21,2048]{2,1,0:T(8,128)(2,1)} %copy-done.3) | data formatting | bytes 688128 | tf_op jit(solution)/shard_map/convert_element_type | solution.py:60
  113.3 1.7 add_multiply_fusion
  115.1 2.2 %fusion.14 = f32[16,84,128]{2,1,0:T(8,128)} fusion(bf16[6,16,128,128]{3,2,1,0:T(8,128)(2,1)S(1)} %bitcast.139, bf16[16,84,128]{2,1,0:T(8,128)(2,1)} %gather_fusion.7, pred[16]{0:T(512)(128)(4,1)S(1)} %copy-done.23), kind=kOutput, calls=%fused_computation.59 | convolution fusion | flops 44212224 | bytes 1556992 | tf_op jit(solution)/shard_map/dot_general | solution.py:22
  117.3 5.1 %reshape.230 = bf16[16,2,5376]{2,1,0:T(2,128)(2,1)} reshape(bf16[2048,4,21]{2,1,0:T(4,128)(2,1)} %bitcast.145) | data formatting | bytes 688128
  122.5 12.0 %all-to-all-start.2 = ((bf16[16,2,5376]{2,1,0:T(2,128)(2,1)}), bf16[16,2,5376]{2,1,0:T(2,128)(2,1)}, u32[]{:S(2)}, u32[]{:S(2)}) async-start(bf16[16,2,5376]{2,1,0:T(2,128)(2,1)} %reshape.230), calls=%async_computation.2 | async-start | bytes 688128 | tf_op jit(solution)/shard_map/all_to_all | solution.py:61
  134.5 2.5 %convolution_add_fusion.4 = f32[16,84,128]{2,1,0:T(8,128)} fusion(f32[16,84,128]{2,1,0:T(8,128)} %fusion.14, bf16[6,16,128,128]{3,2,1,0:T(8,128)(2,1)S(1)} %bitcast.140, bf16[16,84,128]{2,1,0:T(8,128)(2,1)} %gather_fusion.8, pred[16]{0:T(512)(128)(4,1)S(1)} %copy-done.21), kind=kOutput, calls=%fused_computation.18 | convolution fusion | flops 44384256 | bytes 2245120 | tf_op jit(solution)/shard_map/dot_general | solution.py:22
  140.0 2.2 %convolution_add_fusion.2 = f32[16,84,128]{2,1,0:T(8,128)} fusion(f32[16,84,128]{2,1,0:T(8,128)S(1)} %convolution_add_fusion.3, bf16[6,16,128,128]{3,2,1,0:T(8,128)(2,1)S(1)} %bitcast.142, bf16[16,84,128]{2,1,0:T(8,128)(2,1)} %gather_fusion.10, pred[16]{0:T(512)(128)(4,1)S(1)} %copy-done.17), kind=kOutput, calls=%fused_computation.16 | convolution fusion | flops 44384256 | bytes 2277888 | tf_op jit(solution)/shard_map/dot_general | solution.py:22
  142.2 6.9 %all-to-all-done.2 = bf16[16,2,5376]{2,1,0:T(2,128)(2,1)} async-done(((bf16[16,2,5376]{2,1,0:T(2,128)(2,1)}), bf16[16,2,5376]{2,1,0:T(2,128)(2,1)}, u32[]{:S(2)}, u32[]{:S(2)}) %all-to-all-start.2) | async-done | bytes 344096 | tf_op jit(solution)/shard_map/all_to_all | solution.py:61
  149.1 7.1 %reshape.231 = bf16[2048,4,21]{2,1,0:T(4,128)(2,1)} reshape(bf16[16,2,5376]{2,1,0:T(2,128)(2,1)} %all-to-all-done.2) | data formatting | bytes 688128
  156.2 3.4 %copy.112 = bf16[4,21,16,128]{3,2,0,1:T(8,128)(2,1)} copy(bf16[4,21,16,128]{1,0,3,2:T(4,128)(2,1)} %bitcast.147) | data formatting | bytes 688128 | tf_op jit(solution)/shard_map/all_to_all | solution.py:61
  159.6 1.7 fusion.74
  179.2 4.2 %all-to-all-start.3 = ((bf16[4,336,128]{2,0,1:T(4,128)(2,1)}), bf16[4,336,128]{2,0,1:T(4,128)(2,1)}, u32[]{:S(2)}, u32[]{:S(2)}) async-start(bf16[4,336,128]{2,0,1:T(4,128)(2,1)} %copy.104), calls=%async_computation.3 | async-start | bytes 688128 | tf_op jit(solution)/shard_map/all_to_all | solution.py:62
  183.4 2.5 %convolution_add_fusion.1 = f32[16,84,128]{2,1,0:T(8,128)} fusion(f32[16,84,128]{2,1,0:T(8,128)} %convolution_add_fusion.2, bf16[6,16,128,128]{3,2,1,0:T(8,128)(2,1)S(1)} %bitcast.143, bf16[16,84,128]{2,1,0:T(8,128)(2,1)} %gather_fusion.11, pred[16]{0:T(512)(128)(4,1)S(1)} %copy-done.15), kind=kOutput, calls=%fused_computation.15 | convolution fusion | flops 44384256 | bytes 2245120 | tf_op jit(solution)/shard_map/dot_general | solution.py:22
  191.5 4.9 %all-to-all-done.3 = bf16[4,336,128]{2,0,1:T(4,128)(2,1)} async-done(((bf16[4,336,128]{2,0,1:T(4,128)(2,1)}), bf16[4,336,128]{2,0,1:T(4,128)(2,1)}, u32[]{:S(2)}, u32[]{:S(2)}) %all-to-all-start.3) | async-done | bytes 344096 | tf_op jit(solution)/shard_map/all_to_all | solution.py:62
  (138 shorter events, 61.3 us)
Async XLA Ops:
  7.2 80.6 %all-gather.2.cloned.1.call-start = ((), (), s32[]{:S(2)}) async-start(), calls=%async_computation.5 | async-start | bytes 3342336 | tf_op jit(solution)/shard_map/all_gather | solution.py:44
  9.4 17.7 %copy-start.24 = (s32[16,6]{0,1:T(8,128)S(1)}, s32[16,6]{0,1:T(8,128)}, u32[]{:S(2)}) copy-start(s32[16,6]{0,1:T(8,128)} %param.11) | copy-start | bytes 1156
  15.0 26.9 %all-to-all-start = ((bf16[16,2,5376]{2,1,0:T(2,128)(2,1)}), bf16[16,2,5376]{2,1,0:T(2,128)(2,1)S(1)}, u32[]{:S(2)}, u32[]{:S(2)}) async-start(bf16[16,2,5376]{2,1,0:T(2,128)(2,1)} %reshape.228), calls=%async_computation | async-start | bytes 688128 | tf_op jit(solution)/shard_map/all_to_all | solution.py:61
  27.1 60.7 %copy-start.22 = (pred[16]{0:T(512)(128)(4,1)}, pred[16]{0:T(512)(128)(4,1)S(1)}, u32[]{:S(2)}) copy-start(pred[16]{0:T(512)(128)(4,1)S(1)} %get-tuple-element.44) | copy-start | bytes 52
  27.1 62.4 %copy-start.20 = (pred[16]{0:T(512)(128)(4,1)}, pred[16]{0:T(512)(128)(4,1)S(1)}, u32[]{:S(2)}) copy-start(pred[16]{0:T(512)(128)(4,1)S(1)} %get-tuple-element.42) | copy-start | bytes 52
  27.1 63.9 %copy-start.18 = (pred[16]{0:T(512)(128)(4,1)}, pred[16]{0:T(512)(128)(4,1)S(1)}, u32[]{:S(2)}) copy-start(pred[16]{0:T(512)(128)(4,1)S(1)} %get-tuple-element.40) | copy-start | bytes 52
  27.1 65.4 %copy-start.16 = (pred[16]{0:T(512)(128)(4,1)}, pred[16]{0:T(512)(128)(4,1)S(1)}, u32[]{:S(2)}) copy-start(pred[16]{0:T(512)(128)(4,1)S(1)} %get-tuple-element.38) | copy-start | bytes 52
  27.1 65.8 %copy-start.14 = (pred[16]{0:T(512)(128)(4,1)}, pred[16]{0:T(512)(128)(4,1)S(1)}, u32[]{:S(2)}) copy-start(pred[16]{0:T(512)(128)(4,1)S(1)} %get-tuple-element.46) | copy-start | bytes 52
  27.1 66.2 %copy-start.12 = (pred[16]{0:T(512)(128)(4,1)}, pred[16]{0:T(512)(128)(4,1)S(1)}, u32[]{:S(2)}) copy-start(pred[16]{0:T(512)(128)(4,1)S(1)} %get-tuple-element.18) | copy-start | bytes 52
  27.2 21.6 %copy-start.27 = (bf16[1,336,336]{2,1,0:T(8,128)(2,1)S(1)}, bf16[1,336,336]{2,1,0:T(8,128)(2,1)}, u32[]{:S(2)}) copy-start(bf16[1,336,336]{2,1,0:T(8,128)(2,1)} %param.13) | copy-start | bytes 677380
  50.0 14.8 %copy-start.26 = (s32[128]{0:T(128)S(1)}, s32[128]{0:T(128)}, u32[]{:S(2)}) copy-start(s32[128]{0:T(128)} %param.15) | copy-start | bytes 1540
  50.9 21.9 %all-to-all-start.1 = ((bf16[4,336,128]{2,0,1:T(4,128)(2,1)}), bf16[4,336,128]{2,0,1:T(4,128)(2,1)S(1)}, u32[]{:S(2)}, u32[]{:S(2)}) async-start(bf16[4,336,128]{2,0,1:T(4,128)(2,1)} %copy.93), calls=%async_computation.1 | async-start | bytes 688128 | tf_op jit(solution)/shard_map/all_to_all | solution.py:62
  57.1 132.0 %reduce-scatter.2.cloned.1.call-start = ((), (), s32[]{:S(2)}) async-start(), calls=%async_computation.6 | async-start | bytes 208896 | tf_op jit(solution)/shard_map/reduce_scatter | solution.py:67
  57.4 15.5 %copy-start.8 = (s32[1024]{0:T(1024)}, s32[1024]{0:T(1024)S(1)}, u32[]{:S(2)}) copy-start(s32[1024]{0:T(1024)S(1)} %get-tuple-element.52) | copy-start | bytes 12292
  57.4 15.5 %copy-start.9 = (s32[1024]{0:T(1024)}, s32[1024]{0:T(1024)S(1)}, u32[]{:S(2)}) copy-start(s32[1024]{0:T(1024)S(1)} %get-tuple-element.53) | copy-start | bytes 12292
  59.4 14.5 %copy-start.10 = (s32[1024]{0:T(1024)}, s32[1024]{0:T(1024)S(1)}, u32[]{:S(2)}) copy-start(s32[1024]{0:T(1024)S(1)} %get-tuple-element.50) | copy-start | bytes 12292
  62.1 27.4 %copy-start.11 = (s32[1024]{0:T(1024)}, s32[1024]{0:T(1024)S(1)}, u32[]{:S(2)}) copy-start(s32[1024]{0:T(1024)S(1)} %get-tuple-element.49) | copy-start | bytes 12292
  103.5 11.6 %copy-start.23 = (pred[16]{0:T(512)(128)(4,1)S(1)}, pred[16]{0:T(512)(128)(4,1)}, u32[]{:S(2)}) copy-start(pred[16]{0:T(512)(128)(4,1)} %copy-done.22) | copy-start | bytes 52
  113.3 21.2 %copy-start.21 = (pred[16]{0:T(512)(128)(4,1)S(1)}, pred[16]{0:T(512)(128)(4,1)}, u32[]{:S(2)}) copy-start(pred[16]{0:T(512)(128)(4,1)} %copy-done.20) | copy-start | bytes 52
  117.3 21.0 %copy-start.19 = (pred[16]{0:T(512)(128)(4,1)S(1)}, pred[16]{0:T(512)(128)(4,1)}, u32[]{:S(2)}) copy-start(pred[16]{0:T(512)(128)(4,1)} %copy-done.18) | copy-start | bytes 52
  122.5 17.5 %copy-start.17 = (pred[16]{0:T(512)(128)(4,1)S(1)}, pred[16]{0:T(512)(128)(4,1)}, u32[]{:S(2)}) copy-start(pred[16]{0:T(512)(128)(4,1)} %copy-done.16) | copy-start | bytes 52
  122.5 26.7 %all-to-all-start.2 = ((bf16[16,2,5376]{2,1,0:T(2,128)(2,1)}), bf16[16,2,5376]{2,1,0:T(2,128)(2,1)}, u32[]{:S(2)}, u32[]{:S(2)}) async-start(bf16[16,2,5376]{2,1,0:T(2,128)(2,1)} %reshape.230), calls=%async_computation.2 | async-start | bytes 688128 | tf_op jit(solution)/shard_map/all_to_all | solution.py:61
  168.3 15.1 %copy-start.15 = (pred[16]{0:T(512)(128)(4,1)S(1)}, pred[16]{0:T(512)(128)(4,1)}, u32[]{:S(2)}) copy-start(pred[16]{0:T(512)(128)(4,1)} %copy-done.14) | copy-start | bytes 52
  179.2 17.2 %all-to-all-start.3 = ((bf16[4,336,128]{2,0,1:T(4,128)(2,1)}), bf16[4,336,128]{2,0,1:T(4,128)(2,1)}, u32[]{:S(2)}, u32[]{:S(2)}) async-start(bf16[4,336,128]{2,0,1:T(4,128)(2,1)} %copy.104), calls=%async_computation.3 | async-start | bytes 688128 | tf_op jit(solution)/shard_map/all_to_all | solution.py:62
  (10 other events, 42.7 us)
Sparse Core Ops, SparseCore 0:
  10.4 77.3 all-gather.1
  115.2 64.2 reduce-scatter.1
where the time goes:
time: 207 us; the launch traced here: 206 us
  local copies, waits for them, and re-layouts  75.1 us (36%)
  waiting for transfers between devices  48 us (23%)
  starting transfers between devices  33.7 us (16%)
  matrix products  25 us (12%)
  between operations  15.4 us (7%)
  other arithmetic  8.7 us (4%)
    unnamed x62, local copies, waits for them, and re-layouts  25.2 us
    all_to_all x2, starting transfers between devices, per_device(): lax.all_to_all(scaled, 'tm', split_axis=2, concat_axis=1, tiled=True)  23.1 us
    all_to_all x2, waiting for transfers between devices, per_device(): lax.all_to_all(scaled, 'tm', split_axis=2, concat_axis=1, tiled=True)  21.6 us
    dot_general x12, matrix products, network_term(): lax.dot_general(picked, link_blocks[link], (((2,), (1,)), ((0,), (0,))),...  18.5 us
    gather x12, local copies, waits for them, and re-layouts, network_term(): picked = jnp.take(zone_major, zone_links[:, link], axis=0)  15.8 us
    all_gather x1, waiting for transfers between devices, per_device(): all_blocks = lax.all_gather(blocks, 'tm', axis=0, tiled=True)  13.9 us
    all_to_all x2, waiting for transfers between devices, per_device(): lax.all_to_all(temporal_term(moved, masked_turned), 'tm', split_axis=1, c...  11.7 us
    all_to_all x2, starting transfers between devices, per_device(): lax.all_to_all(temporal_term(moved, masked_turned), 'tm', split_axis=1, c...  10.4 us
  transfers between devices with their start and end apart: 6, of which 5 were waited for; matrix products, arithmetic and copies ran while one was open for 38% of the time, Pallas kernels for 0%

commit v1 on v0

--- a/solution.py
+++ b/solution.py
@@ -2,6 +2,7 @@
 import jax.numpy as jnp
 from jax import lax
 from jax.sharding import PartitionSpec as P
+from jax.lax import all_to_all, axis_size
 
 SWEEPS = 2
 
@@ -41,7 +42,14 @@
 
 
 def per_device(cotangent, blocks, zone_links, step_size, coupling, ramp_band, candidates):
-    all_blocks = lax.all_gather(blocks, "tm", axis=0, tiled=True)
+
+    def _find_lane(mine):
+        piece_next = jnp.stack([mine for _ in range(axis_size("tm"))])
+        right_arr = all_to_all(piece_next, "tm", 0, 0)
+        inter = jnp.concatenate(right_arr, axis=0)
+        return inter
+
+    all_blocks = _find_lane(blocks)
     link_blocks = jnp.transpose(all_blocks, (1, 0, 2, 3))
     hour_count = coupling.shape[1]
     hour_ids = jnp.arange(hour_count, dtype=jnp.int32)

time: 207 us -> 258 us (1.25)
  the two profiles are of different devices: /device:TPU:24 before, /device:TPU:48 now
where the time goes in v1:
time: 258 us; the launch traced here: 257 us
  waiting for transfers between devices  89.2 us (35%)
  local copies, waits for them, and re-layouts  79.2 us (31%)
  starting transfers between devices  24.8 us (10%)
  matrix products  21.6 us (8%)
  blocking collectives  17.6 us (7%)
  between operations  15.4 us (6%)
  other arithmetic  8.74 us (3%)
    all_to_all x1, waiting for transfers between devices, _find_lane(): right_arr = all_to_all(piece_next, 'tm', 0, 0)  67 us
    unnamed x66, local copies, waits for them, and re-layouts  25.3 us
    all_to_all x2, waiting for transfers between devices, per_device(): lax.all_to_all(scaled, 'tm', split_axis=2, concat_axis=1, tiled=True)  18.4 us
    all_to_all x1, blocking collectives, per_device(): lax.all_to_all(temporal_term(moved, masked_turned), 'tm', split_axis=1, c...  17.6 us
    gather x12, local copies, waits for them, and re-layouts, network_term(): picked = jnp.take(zone_major, zone_links[:, link], axis=0)  15.9 us
    all_to_all x2, starting transfers between devices, per_device(): lax.all_to_all(scaled, 'tm', split_axis=2, concat_axis=1, tiled=True)  15.4 us
    dot_general x12, matrix products, network_term(): lax.dot_general(picked, link_blocks[link], (((2,), (1,)), ((0,), (0,))),...  15.1 us
    slice x10, local copies, waits for them, and re-layouts, temporal_term(): column = moved[scen, :, 0:bus_width]  7.2 us
  transfers between devices with their start and end apart: 5, of which 4 were waited for; matrix products, arithmetic and copies ran while one was open for 25% of the time, Pallas kernels for 0%

profile of v1, /device:TPU:48, one launch (start us, length us, event | category | flops | bytes accessed | tf_op | source)
XLA Modules:
  0.0 256.6 jit_solution(9436417648071570737)
XLA Ops:
  10.1 4.2 %reshape.235 = bf16[16,2,5376]{2,1,0:T(2,128)(2,1)} reshape(bf16[2048,4,21]{2,1,0:T(4,128)(2,1)S(1)} %bitcast.152) | data formatting | bytes 688128
  14.3 10.1 %all-to-all-start.1 = ((bf16[16,2,5376]{2,1,0:T(2,128)(2,1)}), bf16[16,2,5376]{2,1,0:T(2,128)(2,1)S(1)}, u32[]{:S(2)}, u32[]{:S(2)}) async-start(bf16[16,2,5376]{2,1,0:T(2,128)(2,1)} %reshape.235), calls=%async_computation.1 | async-start | bytes 688128 | tf_op jit(solution)/shard_map/all_to_all | solution.py:69
  25.1 13.4 %all-to-all-done.1 = bf16[16,2,5376]{2,1,0:T(2,128)(2,1)S(1)} async-done(((bf16[16,2,5376]{2,1,0:T(2,128)(2,1)}), bf16[16,2,5376]{2,1,0:T(2,128)(2,1)S(1)}, u32[]{:S(2)}, u32[]{:S(2)}) %all-to-all-start.1) | async-done | bytes 344096 | tf_op jit(solution)/shard_map/all_to_all | solution.py:69
  38.5 5.1 %reshape.236 = bf16[2048,4,21]{2,1,0:T(4,128)(2,1)S(1)} reshape(bf16[16,2,5376]{2,1,0:T(2,128)(2,1)S(1)} %all-to-all-done.1) | data formatting | bytes 688128
  46.8 17.6 %all_to_all.53 = bf16[4,336,128]{2,0,1:T(4,128)(2,1)S(1)} all-to-all(bf16[4,336,128]{2,0,1:T(4,128)(2,1)S(1)} %copy.90), channel_id=1, replica_groups=mesh['scen'=16,'tm'=16] {'tm'}, dimensions={1} | all-to-all | bytes 688128 | tf_op jit(solution)/shard_map/all_to_all | solution.py:70
  64.4 2.5 stack.59
  66.9 4.6 %all-to-all-start = ((bf16[16,1,6,128,128]{4,3,2,1,0:T(8,128)(2,1)}), bf16[16,1,6,128,128]{4,3,2,1,0:T(8,128)(2,1)}, u32[]{:S(2)}, u32[]{:S(2)}) async-start(bf16[16,1,6,128,128]{4,3,2,1,0:T(8,128)(2,1)} %stack.59), calls=%async_computation | async-start | bytes 6291456 | tf_op jit(solution)/shard_map/all_to_all | solution.py:48
  81.9 67.0 %all-to-all-done = bf16[16,1,6,128,128]{4,3,2,1,0:T(8,128)(2,1)} async-done(((bf16[16,1,6,128,128]{4,3,2,1,0:T(8,128)(2,1)}), bf16[16,1,6,128,128]{4,3,2,1,0:T(8,128)(2,1)}, u32[]{:S(2)}, u32[]{:S(2)}) %all-to-all-start) | async-done | bytes 3145760 | tf_op jit(solution)/shard_map/all_to_all | solution.py:48
  148.9 2.2 copy.125
  154.7 2.1 reshape.85
  156.8 2.9 %multiply_reduce_fusion = (f32[21,2048]{1,0:T(8,128)}, f32[21,2048]{1,0:T(8,128)}, f32[4,21,2048]{2,1,0:T(8,128)S(1)}) fusion(f32[2048]{0:T(1024)S(1)} %copy-done.9, f32[4,21,2048]{2,0,1:T(4,128)} %param.9, f32[4,21,2048]{2,1,0:T(8,128)} %reshape.233, f32[4,21,2048]{2,1,0:T(8,128)} %reshape.85), kind=kLoop, calls=%fused_computation.48 | loop fusion | flops 946176 | bytes 3104768 | tf_op jit(solution)/shard_map/reduce_sum | solution.py:66
  169.3 4.0 %copy.95 = bf16[4,21,2048]{1,0,2:T(4,128)(2,1)} copy(bf16[4,21,2048]{2,1,0:T(8,128)(2,1)} %copy-done.2) | data formatting | bytes 688128 | tf_op jit(solution)/shard_map/convert_element_type | solution.py:68
  175.1 2.2 fusion.14
  177.3 5.1 %reshape.237 = bf16[16,2,5376]{2,1,0:T(2,128)(2,1)} reshape(bf16[2048,4,21]{2,1,0:T(4,128)(2,1)} %bitcast.149) | data formatting | bytes 688128
  182.4 5.2 %all-to-all-start.3 = ((bf16[16,2,5376]{2,1,0:T(2,128)(2,1)}), bf16[16,2,5376]{2,1,0:T(2,128)(2,1)}, u32[]{:S(2)}, u32[]{:S(2)}) async-start(bf16[16,2,5376]{2,1,0:T(2,128)(2,1)} %reshape.237), calls=%async_computation.3 | async-start | bytes 688128 | tf_op jit(solution)/shard_map/all_to_all | solution.py:69
  187.7 2.5 convolution_add_fusion.4
  193.2 2.3 convolution_add_fusion.2
  195.4 5.0 %all-to-all-done.3 = bf16[16,2,5376]{2,1,0:T(2,128)(2,1)} async-done(((bf16[16,2,5376]{2,1,0:T(2,128)(2,1)}), bf16[16,2,5376]{2,1,0:T(2,128)(2,1)}, u32[]{:S(2)}, u32[]{:S(2)}) %all-to-all-start.3) | async-done | bytes 344096 | tf_op jit(solution)/shard_map/all_to_all | solution.py:69
  200.4 7.1 %reshape.238 = bf16[2048,4,21]{2,1,0:T(4,128)(2,1)} reshape(bf16[16,2,5376]{2,1,0:T(2,128)(2,1)} %all-to-all-done.3) | data formatting | bytes 688128
  207.5 3.4 %copy.109 = bf16[4,21,16,128]{3,2,0,1:T(8,128)(2,1)} copy(bf16[4,21,16,128]{1,0,3,2:T(4,128)(2,1)} %bitcast.151) | data formatting | bytes 688128 | tf_op jit(solution)/shard_map/all_to_all | solution.py:69
  210.9 1.7 fusion.74
  230.5 4.6 %all-to-all-start.4 = ((bf16[4,336,128]{2,0,1:T(4,128)(2,1)}), bf16[4,336,128]{2,0,1:T(4,128)(2,1)}, u32[]{:S(2)}, u32[]{:S(2)}) async-start(bf16[4,336,128]{2,0,1:T(4,128)(2,1)} %copy.101), calls=%async_computation.4 | async-start | bytes 688128 | tf_op jit(solution)/shard_map/all_to_all | solution.py:70
  235.1 2.5 convolution_add_fusion.1
  243.3 3.8 %all-to-all-done.4 = bf16[4,336,128]{2,0,1:T(4,128)(2,1)} async-done(((bf16[4,336,128]{2,0,1:T(4,128)(2,1)}), bf16[4,336,128]{2,0,1:T(4,128)(2,1)}, u32[]{:S(2)}, u32[]{:S(2)}) %all-to-all-start.4) | async-done | bytes 344096 | tf_op jit(solution)/shard_map/all_to_all | solution.py:70
  (142 shorter events, 60.1 us)
Async XLA Ops:
  14.3 24.2 %all-to-all-start.1 = ((bf16[16,2,5376]{2,1,0:T(2,128)(2,1)}), bf16[16,2,5376]{2,1,0:T(2,128)(2,1)S(1)}, u32[]{:S(2)}, u32[]{:S(2)}) async-start(bf16[16,2,5376]{2,1,0:T(2,128)(2,1)} %reshape.235), calls=%async_computation.1 | async-start | bytes 688128 | tf_op jit(solution)/shard_map/all_to_all | solution.py:69
  25.1 20.3 %copy-start.29 = (bf16[1,336,336]{2,1,0:T(8,128)(2,1)S(1)}, bf16[1,336,336]{2,1,0:T(8,128)(2,1)}, u32[]{:S(2)}) copy-start(bf16[1,336,336]{2,1,0:T(8,128)(2,1)} %param.13) | copy-start | bytes 677380
  45.3 19.1 %copy-start.8 = (bf16[1,6,128,128]{3,2,1,0:T(8,128)(2,1)S(1)}, bf16[1,6,128,128]{3,2,1,0:T(8,128)(2,1)}, u32[]{:S(2)}) copy-start(bf16[1,6,128,128]{3,2,1,0:T(8,128)(2,1)} %param.10) | copy-start | bytes 589828
  66.9 82.0 %all-to-all-start = ((bf16[16,1,6,128,128]{4,3,2,1,0:T(8,128)(2,1)}), bf16[16,1,6,128,128]{4,3,2,1,0:T(8,128)(2,1)}, u32[]{:S(2)}, u32[]{:S(2)}) async-start(bf16[16,1,6,128,128]{4,3,2,1,0:T(8,128)(2,1)} %stack.59), calls=%async_computation | async-start | bytes 6291456 | tf_op jit(solution)/shard_map/all_to_all | solution.py:48
  71.5 8.2 %copy-start.28 = (s32[128]{0:T(128)S(1)}, s32[128]{0:T(128)}, u32[]{:S(2)}) copy-start(s32[128]{0:T(128)} %param.15) | copy-start | bytes 1540
  71.5 169.3 %reduce-scatter.2.cloned.1.call-start = ((), (), s32[]{:S(2)}) async-start(), calls=%async_computation.6 | async-start | bytes 208896 | tf_op jit(solution)/shard_map/reduce_scatter | solution.py:75
  72.1 79.0 %copy-start.24 = (pred[16]{0:T(512)(128)(4,1)}, pred[16]{0:T(512)(128)(4,1)S(1)}, u32[]{:S(2)}) copy-start(pred[16]{0:T(512)(128)(4,1)S(1)} %get-tuple-element.44) | copy-start | bytes 52
  72.1 79.4 %copy-start.22 = (pred[16]{0:T(512)(128)(4,1)}, pred[16]{0:T(512)(128)(4,1)S(1)}, u32[]{:S(2)}) copy-start(pred[16]{0:T(512)(128)(4,1)S(1)} %get-tuple-element.42) | copy-start | bytes 52
  72.1 79.8 %copy-start.20 = (pred[16]{0:T(512)(128)(4,1)}, pred[16]{0:T(512)(128)(4,1)S(1)}, u32[]{:S(2)}) copy-start(pred[16]{0:T(512)(128)(4,1)S(1)} %get-tuple-element.40) | copy-start | bytes 52
  72.1 80.3 %copy-start.18 = (pred[16]{0:T(512)(128)(4,1)}, pred[16]{0:T(512)(128)(4,1)S(1)}, u32[]{:S(2)}) copy-start(pred[16]{0:T(512)(128)(4,1)S(1)} %get-tuple-element.38) | copy-start | bytes 52
  72.1 80.7 %copy-start.16 = (pred[16]{0:T(512)(128)(4,1)}, pred[16]{0:T(512)(128)(4,1)S(1)}, u32[]{:S(2)}) copy-start(pred[16]{0:T(512)(128)(4,1)S(1)} %get-tuple-element.46) | copy-start | bytes 52
  72.1 81.2 %copy-start.14 = (pred[16]{0:T(512)(128)(4,1)}, pred[16]{0:T(512)(128)(4,1)S(1)}, u32[]{:S(2)}) copy-start(pred[16]{0:T(512)(128)(4,1)S(1)} %get-tuple-element.18) | copy-start | bytes 52
  72.2 8.7 %copy-start.10 = (s32[1024]{0:T(1024)}, s32[1024]{0:T(1024)S(1)}, u32[]{:S(2)}) copy-start(s32[1024]{0:T(1024)S(1)} %get-tuple-element.52) | copy-start | bytes 12292
  72.2 8.6 %copy-start.11 = (s32[1024]{0:T(1024)}, s32[1024]{0:T(1024)S(1)}, u32[]{:S(2)}) copy-start(s32[1024]{0:T(1024)S(1)} %get-tuple-element.53) | copy-start | bytes 12292
  74.2 6.7 %copy-start.12 = (s32[1024]{0:T(1024)}, s32[1024]{0:T(1024)S(1)}, u32[]{:S(2)}) copy-start(s32[1024]{0:T(1024)S(1)} %get-tuple-element.50) | copy-start | bytes 12292
  163.4 11.6 %copy-start.25 = (pred[16]{0:T(512)(128)(4,1)S(1)}, pred[16]{0:T(512)(128)(4,1)}, u32[]{:S(2)}) copy-start(pred[16]{0:T(512)(128)(4,1)} %copy-done.24) | copy-start | bytes 52
  173.3 14.4 %copy-start.23 = (pred[16]{0:T(512)(128)(4,1)S(1)}, pred[16]{0:T(512)(128)(4,1)}, u32[]{:S(2)}) copy-start(pred[16]{0:T(512)(128)(4,1)} %copy-done.22) | copy-start | bytes 52
  177.3 14.2 %copy-start.21 = (pred[16]{0:T(512)(128)(4,1)S(1)}, pred[16]{0:T(512)(128)(4,1)}, u32[]{:S(2)}) copy-start(pred[16]{0:T(512)(128)(4,1)} %copy-done.20) | copy-start | bytes 52
  182.4 10.7 %copy-start.19 = (pred[16]{0:T(512)(128)(4,1)S(1)}, pred[16]{0:T(512)(128)(4,1)}, u32[]{:S(2)}) copy-start(pred[16]{0:T(512)(128)(4,1)} %copy-done.18) | copy-start | bytes 52
  182.4 18.0 %all-to-all-start.3 = ((bf16[16,2,5376]{2,1,0:T(2,128)(2,1)}), bf16[16,2,5376]{2,1,0:T(2,128)(2,1)}, u32[]{:S(2)}, u32[]{:S(2)}) async-start(bf16[16,2,5376]{2,1,0:T(2,128)(2,1)} %reshape.237), calls=%async_computation.3 | async-start | bytes 688128 | tf_op jit(solution)/shard_map/all_to_all | solution.py:69
  219.6 15.5 %copy-start.17 = (pred[16]{0:T(512)(128)(4,1)S(1)}, pred[16]{0:T(512)(128)(4,1)}, u32[]{:S(2)}) copy-start(pred[16]{0:T(512)(128)(4,1)} %copy-done.16) | copy-start | bytes 52
  228.2 10.7 %copy-start.15 = (pred[16]{0:T(512)(128)(4,1)S(1)}, pred[16]{0:T(512)(128)(4,1)}, u32[]{:S(2)}) copy-start(pred[16]{0:T(512)(128)(4,1)} %copy-done.14) | copy-start | bytes 52
  230.5 16.6 %all-to-all-start.4 = ((bf16[4,336,128]{2,0,1:T(4,128)(2,1)}), bf16[4,336,128]{2,0,1:T(4,128)(2,1)}, u32[]{:S(2)}, u32[]{:S(2)}) async-start(bf16[4,336,128]{2,0,1:T(4,128)(2,1)} %copy.101), calls=%async_computation.4 | async-start | bytes 688128 | tf_op jit(solution)/shard_map/all_to_all | solution.py:70
  240.7 7.6 %copy-start.1 = (f32[4,21,2048]{2,1,0:T(8,128)S(1)}, f32[4,21,2048]{2,1,0:T(8,128)}, u32[]{:S(2)}) copy-start(f32[4,21,2048]{2,1,0:T(8,128)} %copy-done) | copy-start | bytes 2064388
  (11 other events, 26.5 us)
Sparse Core Ops, SparseCore 0:
  175.2 54.4 reduce-scatter.1
